TPU v7x, 32 devices: a whole 2x2x4 slice. The times are simulated.
32 devices in a mesh: src: 8 (over y, x, core), tgt: 4 (over z).
Axes of the slice: x: 2, y: 2, z: 4, core: 2. Of those that a mesh axis runs over, the one named last changes fastest.
Arguments:
- src_emb: bfloat16 [64, 131072], P(None, 'src'), may hold values from -3 to 3
- tgt_emb: bfloat16 [64, 65536], P(None, 'tgt'), may hold values from -3 to 3
- src_hidden: bfloat16 [64, 131072], P(None, 'src'), may hold values from -4 to 4
- growth: float32 [131072], P('src'), may hold values from -1 to 1
- tgt_mass: float32 [65536], P('tgt'), may hold values from 0.5 to 2
- pair_code: int32 [8, 4, 512], P('src', 'tgt'), may hold values from 0 to 16383, as said below
- pair_count: int32 [8, 4], P('src', 'tgt'), may hold values from 128 to 512, as said below
- block_batch: int32 [1024], P('src'), may hold values from 0 to 31
Outputs:
- src_potential: float32 [131072], P('src')
- tgt_potential: float32 [65536], P('tgt')
- tgt_grad: float32 [64, 65536], P(None, 'tgt')
- adapter_grad: float32 [32, 64, 64], P(('src', 'tgt'))
Inputs may be any that keep to these rules, and one draw needn't show every extreme that they name: `pair_code`: the codes of one device are distinct; among the first 128 entries of each device's list every one of its 128 source blocks and every one of its 128 target blocks appears. `pair_count`: in every draw some device has all 512 entries live.
All inputs are finite; a program needn't handle non-finite values.
Results may differ from a plain program's by a relative error of at most 0.0003.
Values sent between devices are 32-bit elements; how exact they have to be, the bound alone decides.
A program may use at most 192 MiB of HBM per device.

v0:
```python
import math

import jax
import jax.numpy as jnp
from jax import lax
from jax.sharding import PartitionSpec as P

BLK = 128
ENC_DEV = 1
ITERS = 2


entropy_scale = 0.5
update_power = 0.4
highest = lax.Precision.HIGHEST


def rescale(scaling, masses, totals):
    return jnp.sqrt(scaling) * jnp.power(masses / totals, update_power)


def pick_blocks(selector, blocks):
    picked = jnp.einsum(
        "gb,dbi->dgi", selector.astype(jnp.bfloat16), blocks, preferred_element_type=jnp.float32
    )
    return picked.astype(jnp.bfloat16)


def per_device(src_emb, tgt_emb, src_hidden, growth, tgt_mass, pair_code, pair_count, block_batch):
    feat_width = src_emb.shape[0]
    src_blocks = src_emb.shape[1] // BLK
    tgt_blocks = tgt_emb.shape[1] // BLK
    src_cells = src_blocks * BLK
    tgt_cells = tgt_blocks * BLK
    slot_count = pair_code.shape[2]
    group_size = math.gcd(slot_count, 64)
    group_count = slot_count // group_size
    pair_slots = pair_code.reshape(slot_count)
    alive_mask = (jnp.arange(slot_count, dtype=jnp.int32) < pair_count.reshape(())).astype(
        jnp.float32
    )
    src_ids = pair_slots // tgt_blocks
    tgt_ids = pair_slots % tgt_blocks
    src_select = (src_ids[:, None] == jnp.arange(src_blocks, dtype=jnp.int32)[None, :]).astype(
        jnp.float32
    )
    tgt_select = (tgt_ids[:, None] == jnp.arange(tgt_blocks, dtype=jnp.int32)[None, :]).astype(
        jnp.float32
    )
    x_blocks = src_emb.reshape(feat_width, src_blocks, BLK)
    y_blocks = tgt_emb.reshape(feat_width, tgt_blocks, BLK)
    x_norms = jnp.sum(jnp.square(x_blocks.astype(jnp.float32)), axis=0)
    y_norms = jnp.sum(jnp.square(y_blocks.astype(jnp.float32)), axis=0)
    src_sel_groups = src_select.reshape(group_count, group_size, src_blocks)
    tgt_sel_groups = tgt_select.reshape(group_count, group_size, tgt_blocks)

    def kernel_group(inputs):
        src_sel, tgt_sel, alive_group = inputs
        x_part = pick_blocks(src_sel, x_blocks)
        y_part = pick_blocks(tgt_sel, y_blocks)
        inner_prods = jnp.einsum("dgi,dgj->gij", x_part, y_part, preferred_element_type=jnp.float32)
        x_sq = jnp.dot(src_sel, x_norms, precision=highest)
        y_sq = jnp.dot(tgt_sel, y_norms, precision=highest)
        distance = (x_sq[:, :, None] + y_sq[:, None, :] - 2.0 * inner_prods) / feat_width
        return jnp.exp(-distance / entropy_scale) * alive_group[:, None, None]

    kernel = lax.map(
        kernel_group, (src_sel_groups, tgt_sel_groups, alive_mask.reshape(group_count, group_size))
    )
    kernel = kernel.reshape(slot_count, BLK, BLK)
    src_mass = jnp.exp(growth)
    src_scale = jnp.ones((src_cells,), jnp.float32)
    tgt_scale = jnp.ones((tgt_cells,), jnp.float32)
    for iteration in range(ITERS):
        tgt_picked = jnp.dot(tgt_select, tgt_scale.reshape(tgt_blocks, BLK), precision=highest)
        src_picked = jnp.dot(src_select, src_scale.reshape(src_blocks, BLK), precision=highest)
        row_slots = jnp.einsum("pij,pj->pi", kernel, tgt_picked, precision=highest)
        col_slots = jnp.einsum("pij,pi->pj", kernel, src_picked, precision=highest)
        row_part = jnp.dot(src_select.T, row_slots, precision=highest).reshape(src_cells)
        col_part = jnp.dot(tgt_select.T, col_slots, precision=highest).reshape(tgt_cells)
        row_sums = lax.psum(row_part, "tgt")
        col_sums = lax.psum(col_part, "src")
        src_scale, tgt_scale = (
            rescale(src_scale, src_mass, row_sums),
            rescale(tgt_scale, tgt_mass, col_sums),
        )
    src_potential = entropy_scale * jnp.log(src_scale)
    tgt_potential = entropy_scale * jnp.log(tgt_scale)
    src_blocked = src_scale.reshape(src_blocks, BLK)
    tgt_blocked = tgt_scale.reshape(tgt_blocks, BLK)

    def gradient_group(carry, inputs):
        dx_total, dy_total = carry
        src_sel, tgt_sel, kernel_part = inputs
        row_scale = jnp.dot(src_sel, src_blocked, precision=highest)
        col_scale = jnp.dot(tgt_sel, tgt_blocked, precision=highest)
        transport = row_scale[:, :, None] * kernel_part * col_scale[:, None, :]
        plan_bf16 = transport.astype(jnp.bfloat16)
        x_part = pick_blocks(src_sel, x_blocks)
        y_part = pick_blocks(tgt_sel, y_blocks)
        pulled = jnp.einsum("gij,dgj->dgi", plan_bf16, y_part, preferred_element_type=jnp.float32)
        pushed = jnp.einsum("gij,dgi->dgj", plan_bf16, x_part, preferred_element_type=jnp.float32)
        dx_term = jnp.sum(transport, axis=2)[None] * x_part.astype(jnp.float32) - pulled
        dy_term = jnp.sum(transport, axis=1)[None] * y_part.astype(jnp.float32) - pushed
        dx_total = dx_total + jnp.einsum("gb,dgi->dbi", src_sel, dx_term, precision=highest)
        dy_total = dy_total + jnp.einsum("gb,dgi->dbi", tgt_sel, dy_term, precision=highest)
        return ((dx_total, dy_total), None)

    start_grads = (
        jnp.zeros((feat_width, src_blocks, BLK), jnp.float32),
        jnp.zeros((feat_width, tgt_blocks, BLK), jnp.float32),
    )
    (dx_total, dy_total), _ = lax.scan(
        gradient_group,
        start_grads,
        (src_sel_groups, tgt_sel_groups, kernel.reshape(group_count, group_size, BLK, BLK)),
    )
    tgt_grad = lax.psum(dy_total.reshape(feat_width, tgt_cells), "src")
    hidden_blocks = src_hidden.reshape(feat_width, src_blocks, BLK)
    grad_share = lax.psum_scatter(dx_total, "tgt", scatter_dimension=1, tiled=True)
    share_blocks = grad_share.shape[1]
    first_block = lax.axis_index("tgt") * share_blocks
    hidden_share = lax.dynamic_slice_in_dim(hidden_blocks, first_block, share_blocks, 1)
    batch_share = lax.dynamic_slice_in_dim(block_batch, first_block, share_blocks, 0)
    outer = (
        jnp.einsum("dbi,ebi->bde", hidden_share.astype(jnp.float32), grad_share, precision=highest)
        / BLK
    )
    wanted = jnp.arange(ENC_DEV * lax.axis_size(("src", "tgt")), dtype=jnp.int32)
    owners = (batch_share[None, :] == wanted[:, None]).astype(jnp.float32)
    adapter_grad = lax.psum_scatter(
        jnp.einsum("kb,bde->kde", owners, outer, precision=highest),
        ("src", "tgt"),
        scatter_dimension=0,
        tiled=True,
    )
    return (src_potential, tgt_potential, tgt_grad, adapter_grad)


def solution(mesh):
    in_specs = (
        P(None, "src"),
        P(None, "tgt"),
        P(None, "src"),
        P("src"),
        P("tgt"),
        P("src", "tgt", None),
        P("src", "tgt"),
        P("src"),
    )
    out_specs = (P("src"), P("tgt"), P(None, "tgt"), P(("src", "tgt"), None, None))
    return jax.shard_map(
        per_device, mesh=mesh, in_specs=in_specs, out_specs=out_specs, check_vma=False
    )
```

profile of v0, /device:TPU:0, one launch (start us, length us, event | category | flops | bytes accessed | tf_op | source)
XLA Modules:
  0.0 1027.3 jit_solution(16935787503366914984)
XLA Ops:
  17.6 84.6 %while.23 = (s32[]{:T(128)}, f32[8,64,128,128]{3,2,1,0:T(8,128)}, f32[8,64,128]{2,1,0:T(8,128)S(1)}, f32[128,128]{1,0:T(8,128)S(1)}, f32[8,64,128]{2,1,0:T(8,128...) while((s32[]{:T(128)}, f32[8,64,128,128]{3,2,1,0:T(8,128)}, ...), condition=%wide.region_3.4_spmd, body=%wide.region_2.3_spmd.sunk | while | flops 435159040 | bytes 21334412 | solution.py:67
  102.5 55.7 %fusion.97 = f32[512,1,128]{2,1,0:T(1,128)S(1)} fusion(f32[512,128,128]{2,1,0:T(8,128)} %bitcast.228, f32[512,128,1]{1,2,0:T(1,128)S(1)} %bitcast.246), kind=kOutput, calls=%fused_computation.137 | convolution fusion | flops 100663296 | bytes 34078720 | tf_op jit(solution)/shard_map/pij,pj->pi/dot_general | solution.py:77
  160.0 32.0 %fusion.98 = f32[512,1,128]{2,1,0:T(1,128)S(1)} fusion(f32[512,128,128]{2,1,0:T(8,128)} %bitcast.229, f32[512,128,1]{1,2,0:T(1,128)S(1)} %bitcast.248), kind=kOutput, calls=%fused_computation.138 | convolution fusion | flops 100663296 | bytes 34078720 | tf_op jit(solution)/shard_map/pij,pi->pj/dot_general | solution.py:78
  197.7 32.3 %fusion.100 = f32[512,1,128]{2,1,0:T(1,128)S(1)} fusion(f32[512,128,128]{2,1,0:T(8,128)} %bitcast.230, f32[512,128,1]{1,2,0:T(1,128)S(1)} %bitcast.249), kind=kOutput, calls=%fused_computation.140 | convolution fusion | flops 100663296 | bytes 34078720 | tf_op jit(solution)/shard_map/pij,pi->pj/dot_general | solution.py:78
  231.3 53.3 %all-reduce.12.cloned.1.call-done = (f32[16384]{0:T(1024)}, f32[16384]{0:T(1024)}) async-done(((f32[16384]{0:T(1024)}, f32[16384]{0:T(1024)}), (f32[16384]{0:T(1024)}, f32[16384]{0:T(1024)})) %all-reduce.12.cloned.1.call-update) | async-done | bytes 131088 | tf_op jit(solution)/shard_map/psum | solution.py:82
  285.8 55.9 %fusion.99 = f32[512,1,128]{2,1,0:T(1,128)S(1)} fusion(f32[512,128,128]{2,1,0:T(8,128)} %bitcast.231, f32[512,128,1]{1,2,0:T(1,128)S(1)} %bitcast.247), kind=kOutput, calls=%fused_computation.139 | convolution fusion | flops 100663296 | bytes 34078720 | tf_op jit(solution)/shard_map/pij,pj->pi/dot_general | solution.py:77
  343.7 33.0 %all-reduce.8.cloned.1.call-done = f32[16384]{0:T(1024)} async-done(((f32[16384]{0:T(1024)}), f32[16384]{0:T(1024)}) %all-reduce.8.cloned.1.call-update) | async-done | bytes 65552 | tf_op jit(solution)/shard_map/psum | solution.py:81
  378.3 330.9 %while.24 = (s32[]{:T(128)}, f32[64,128,128]{1,2,0:T(8,128)}, f32[64,128,128]{1,2,0:T(8,128)}, f32[8,64,128]{2,1,0:T(8,128)S(1)}, f32[128,128]{1,0:T(8,128)}, /*...) while((s32[]{:T(128)}, f32[64,128,128]{1,2,0:T(8,128)}, ...), condition=%wide.region_11.12_spmd.clone, body=%wide.region_8.11_spmd.clone.sunk | while | flops 2191507456 | bytes 61508292 | solution.py:113
  432.3 11.2 %bitcast_add_fusion.5 = f32[64,128,128]{1,2,0:T(8,128)} fusion(f32[64,128,128]{1,2,0:T(8,128)} %get-tuple-element.360, f32[64,64,128]{2,1,0:T(8,128)} %fusion.193, bf16[64,64,128]{2,1,0:T(8,128)(2,1)} %fusion.187, pred[]{:T(512)S(6)} %compare.16, f32[64,128]{1,0:T(8,128)S(1)} %get-tuple-element.315, f32[8,64,128]{2,1,0:T(8,128)} %get-tuple-element.376, ...), kind=kOutput, calls=%fused_computation.23.clone.1 | convolution fusion | flops 808976384 | bytes 11600385 | tf_op jit(solution)/shard_map/while/body/eval_jaxpr/gb,dgi->dbi/dot_general | solution.py:106
  448.2 11.3 %bitcast_add_fusion.4 = f32[64,128,128]{1,2,0:T(8,128)} fusion(f32[64,128,128]{1,2,0:T(8,128)} %get-tuple-element.359, f32[64,64,128]{2,1,0:T(8,128)S(1)} %fusion.190, bf16[64,64,128]{2,1,0:T(8,128)(2,1)S(1)} %fusion.191, pred[]{:T(512)S(6)} %compare.16, f32[64,128]{1,0:T(8,128)S(1)} %get-tuple-element.314, ...), kind=kOutput, calls=%fused_computation.24.clone.1 | convolution fusion | flops 808976384 | bytes 11599877 | tf_op jit(solution)/shard_map/while/body/eval_jaxpr/gb,dgi->dbi/dot_general | solution.py:105
  473.9 11.2 %bitcast_add_fusion.5 = f32[64,128,128]{1,2,0:T(8,128)} fusion(f32[64,128,128]{1,2,0:T(8,128)} %get-tuple-element.360, f32[64,64,128]{2,1,0:T(8,128)} %fusion.193, bf16[64,64,128]{2,1,0:T(8,128)(2,1)} %fusion.187, pred[]{:T(512)S(6)} %compare.16, f32[64,128]{1,0:T(8,128)S(1)} %get-tuple-element.315, f32[8,64,128]{2,1,0:T(8,128)} %get-tuple-element.376, ...), kind=kOutput, calls=%fused_computation.23.clone.1 | convolution fusion | flops 808976384 | bytes 11600385 | tf_op jit(solution)/shard_map/while/body/eval_jaxpr/gb,dgi->dbi/dot_general | solution.py:106
  489.8 11.3 %bitcast_add_fusion.4 = f32[64,128,128]{1,2,0:T(8,128)} fusion(f32[64,128,128]{1,2,0:T(8,128)} %get-tuple-element.359, f32[64,64,128]{2,1,0:T(8,128)S(1)} %fusion.190, bf16[64,64,128]{2,1,0:T(8,128)(2,1)S(1)} %fusion.191, pred[]{:T(512)S(6)} %compare.16, f32[64,128]{1,0:T(8,128)S(1)} %get-tuple-element.314, ...), kind=kOutput, calls=%fused_computation.24.clone.1 | convolution fusion | flops 808976384 | bytes 11599877 | tf_op jit(solution)/shard_map/while/body/eval_jaxpr/gb,dgi->dbi/dot_general | solution.py:105
  515.5 11.2 %bitcast_add_fusion.5 = f32[64,128,128]{1,2,0:T(8,128)} fusion(f32[64,128,128]{1,2,0:T(8,128)} %get-tuple-element.360, f32[64,64,128]{2,1,0:T(8,128)} %fusion.193, bf16[64,64,128]{2,1,0:T(8,128)(2,1)} %fusion.187, pred[]{:T(512)S(6)} %compare.16, f32[64,128]{1,0:T(8,128)S(1)} %get-tuple-element.315, f32[8,64,128]{2,1,0:T(8,128)} %get-tuple-element.376, ...), kind=kOutput, calls=%fused_computation.23.clone.1 | convolution fusion | flops 808976384 | bytes 11600385 | tf_op jit(solution)/shard_map/while/body/eval_jaxpr/gb,dgi->dbi/dot_general | solution.py:106
  531.4 11.3 %bitcast_add_fusion.4 = f32[64,128,128]{1,2,0:T(8,128)} fusion(f32[64,128,128]{1,2,0:T(8,128)} %get-tuple-element.359, f32[64,64,128]{2,1,0:T(8,128)S(1)} %fusion.190, bf16[64,64,128]{2,1,0:T(8,128)(2,1)S(1)} %fusion.191, pred[]{:T(512)S(6)} %compare.16, f32[64,128]{1,0:T(8,128)S(1)} %get-tuple-element.314, ...), kind=kOutput, calls=%fused_computation.24.clone.1 | convolution fusion | flops 808976384 | bytes 11599877 | tf_op jit(solution)/shard_map/while/body/eval_jaxpr/gb,dgi->dbi/dot_general | solution.py:105
  557.0 11.2 %bitcast_add_fusion.5 = f32[64,128,128]{1,2,0:T(8,128)} fusion(f32[64,128,128]{1,2,0:T(8,128)} %get-tuple-element.360, f32[64,64,128]{2,1,0:T(8,128)} %fusion.193, bf16[64,64,128]{2,1,0:T(8,128)(2,1)} %fusion.187, pred[]{:T(512)S(6)} %compare.16, f32[64,128]{1,0:T(8,128)S(1)} %get-tuple-element.315, f32[8,64,128]{2,1,0:T(8,128)} %get-tuple-element.376, ...), kind=kOutput, calls=%fused_computation.23.clone.1 | convolution fusion | flops 808976384 | bytes 11600385 | tf_op jit(solution)/shard_map/while/body/eval_jaxpr/gb,dgi->dbi/dot_general | solution.py:106
  572.9 11.3 %bitcast_add_fusion.4 = f32[64,128,128]{1,2,0:T(8,128)} fusion(f32[64,128,128]{1,2,0:T(8,128)} %get-tuple-element.359, f32[64,64,128]{2,1,0:T(8,128)S(1)} %fusion.190, bf16[64,64,128]{2,1,0:T(8,128)(2,1)S(1)} %fusion.191, pred[]{:T(512)S(6)} %compare.16, f32[64,128]{1,0:T(8,128)S(1)} %get-tuple-element.314, ...), kind=kOutput, calls=%fused_computation.24.clone.1 | convolution fusion | flops 808976384 | bytes 11599877 | tf_op jit(solution)/shard_map/while/body/eval_jaxpr/gb,dgi->dbi/dot_general | solution.py:105
  598.6 11.2 %bitcast_add_fusion.5 = f32[64,128,128]{1,2,0:T(8,128)} fusion(f32[64,128,128]{1,2,0:T(8,128)} %get-tuple-element.360, f32[64,64,128]{2,1,0:T(8,128)} %fusion.193, bf16[64,64,128]{2,1,0:T(8,128)(2,1)} %fusion.187, pred[]{:T(512)S(6)} %compare.16, f32[64,128]{1,0:T(8,128)S(1)} %get-tuple-element.315, f32[8,64,128]{2,1,0:T(8,128)} %get-tuple-element.376, ...), kind=kOutput, calls=%fused_computation.23.clone.1 | convolution fusion | flops 808976384 | bytes 11600385 | tf_op jit(solution)/shard_map/while/body/eval_jaxpr/gb,dgi->dbi/dot_general | solution.py:106
  614.5 11.3 %bitcast_add_fusion.4 = f32[64,128,128]{1,2,0:T(8,128)} fusion(f32[64,128,128]{1,2,0:T(8,128)} %get-tuple-element.359, f32[64,64,128]{2,1,0:T(8,128)S(1)} %fusion.190, bf16[64,64,128]{2,1,0:T(8,128)(2,1)S(1)} %fusion.191, pred[]{:T(512)S(6)} %compare.16, f32[64,128]{1,0:T(8,128)S(1)} %get-tuple-element.314, ...), kind=kOutput, calls=%fused_computation.24.clone.1 | convolution fusion | flops 808976384 | bytes 11599877 | tf_op jit(solution)/shard_map/while/body/eval_jaxpr/gb,dgi->dbi/dot_general | solution.py:105
  640.2 11.2 %bitcast_add_fusion.5 = f32[64,128,128]{1,2,0:T(8,128)} fusion(f32[64,128,128]{1,2,0:T(8,128)} %get-tuple-element.360, f32[64,64,128]{2,1,0:T(8,128)} %fusion.193, bf16[64,64,128]{2,1,0:T(8,128)(2,1)} %fusion.187, pred[]{:T(512)S(6)} %compare.16, f32[64,128]{1,0:T(8,128)S(1)} %get-tuple-element.315, f32[8,64,128]{2,1,0:T(8,128)} %get-tuple-element.376, ...), kind=kOutput, calls=%fused_computation.23.clone.1 | convolution fusion | flops 808976384 | bytes 11600385 | tf_op jit(solution)/shard_map/while/body/eval_jaxpr/gb,dgi->dbi/dot_general | solution.py:106
  656.1 11.3 %bitcast_add_fusion.4 = f32[64,128,128]{1,2,0:T(8,128)} fusion(f32[64,128,128]{1,2,0:T(8,128)} %get-tuple-element.359, f32[64,64,128]{2,1,0:T(8,128)S(1)} %fusion.190, bf16[64,64,128]{2,1,0:T(8,128)(2,1)S(1)} %fusion.191, pred[]{:T(512)S(6)} %compare.16, f32[64,128]{1,0:T(8,128)S(1)} %get-tuple-element.314, ...), kind=kOutput, calls=%fused_computation.24.clone.1 | convolution fusion | flops 808976384 | bytes 11599877 | tf_op jit(solution)/shard_map/while/body/eval_jaxpr/gb,dgi->dbi/dot_general | solution.py:105
  697.7 11.3 %bitcast_add_fusion.4 = f32[64,128,128]{1,2,0:T(8,128)} fusion(f32[64,128,128]{1,2,0:T(8,128)} %get-tuple-element.359, f32[64,64,128]{2,1,0:T(8,128)S(1)} %fusion.190, bf16[64,64,128]{2,1,0:T(8,128)(2,1)S(1)} %fusion.191, pred[]{:T(512)S(6)} %compare.16, f32[64,128]{1,0:T(8,128)S(1)} %get-tuple-element.314, ...), kind=kOutput, calls=%fused_computation.24.clone.1 | convolution fusion | flops 808976384 | bytes 11599877 | tf_op jit(solution)/shard_map/while/body/eval_jaxpr/gb,dgi->dbi/dot_general | solution.py:105
  729.5 61.7 %reduce-scatter.3.cloned.1.call-done = f32[64,32,128]{2,0,1:T(8,128)} async-done(((f32[64,128,128]{2,0,1:T(8,128)}), f32[64,32,128]{2,0,1:T(8,128)}) %reduce-scatter.3.cloned.1.call-update) | async-done | bytes 1048592 | tf_op jit(solution)/shard_map/reduce_scatter | solution.py:120
  796.3 79.4 %all-reduce.10.cloned.1.call-done = f32[64,16384]{1,0:T(8,128)} async-done(((f32[64,16384]{1,0:T(8,128)}), f32[64,16384]{1,0:T(8,128)}) %all-reduce.10.cloned.1.call-update) | async-done | bytes 4194320 | tf_op jit(solution)/shard_map/psum | solution.py:118
  875.7 139.8 %reduce-scatter.5.cloned.1.call-done = f32[1,64,64]{2,1,0:T(8,128)} async-done(((f32[32,64,64]{2,1,0:T(8,128)}), f32[1,64,64]{2,1,0:T(8,128)}) %reduce-scatter.5.cloned.1.call-update) | async-done | bytes 16400 | tf_op jit(solution)/shard_map/reduce_scatter | solution.py:131
  (218 shorter events, 321.8 us)
Async XLA Ops:
  7.2 189.4 %all-reduce.6.cloned.1.call-start = ((), (), s32[]{:S(2)}) async-start(), calls=%async_computation.2 | async-start | bytes 131072 | tf_op jit(solution)/shard_map/psum | solution.py:81
  17.6 84.6 %copy-start.9 = (s32[1,1,512]{2,1,0:T(1,128)S(1)}, s32[1,1,512]{2,1,0:T(1,128)}, u32[]{:S(2)}) copy-start(s32[1,1,512]{2,1,0:T(1,128)} %param.17) | copy-start | bytes 6148
  159.4 125.2 %all-reduce.12.cloned.1.call-start = ((), (), s32[]{:S(2)}) async-start(), calls=%async_computation.7 | async-start | bytes 262144 | tf_op jit(solution)/shard_map/psum | solution.py:82
  160.0 36.6 %copy-start.5 = (f32[16384]{0:T(1024)S(1)}, f32[16384]{0:T(1024)}, u32[]{:S(2)}) copy-start(f32[16384]{0:T(1024)} %param.15) | copy-start | bytes 196612
  197.7 86.9 %copy-start.4 = (f32[16384]{0:T(1024)S(1)}, f32[16384]{0:T(1024)}, u32[]{:S(2)}) copy-start(f32[16384]{0:T(1024)} %param.16) | copy-start | bytes 196612
  231.2 145.4 %all-reduce.8.cloned.1.call-start = ((), (), s32[]{:S(2)}) async-start(), calls=%async_computation.3 | async-start | bytes 131072 | tf_op jit(solution)/shard_map/psum | solution.py:81
  285.8 57.1 %copy-start.7 = (f32[16384]{0:T(1024)S(1)}, f32[16384]{0:T(1024)}, u32[]{:S(2)}) copy-start(f32[16384]{0:T(1024)} %get-tuple-element.184) | copy-start | bytes 196612
  285.8 57.1 %copy-start.8 = (f32[16384]{0:T(1024)S(1)}, f32[16384]{0:T(1024)}, u32[]{:S(2)}) copy-start(f32[16384]{0:T(1024)} %get-tuple-element.185) | copy-start | bytes 196612
  285.8 90.9 %copy-start.6 = (f32[16384]{0:T(1024)S(1)}, f32[16384]{0:T(1024)}, u32[]{:S(2)}) copy-start(f32[16384]{0:T(1024)} %all-reduce.6.cloned.1.call-done) | copy-start | bytes 196612
  342.8 448.4 %reduce-scatter.3.cloned.1.call-start = ((), (), s32[]{:S(2)}) async-start(), calls=%async_computation.5 | async-start | bytes 5242880 | tf_op jit(solution)/shard_map/reduce_scatter | solution.py:120
  392.9 10.6 %copy-start.2 = (bf16[64,64,128]{2,1,0:T(8,128)(2,1)S(1)}, bf16[64,64,128]{2,1,0:T(8,128)(2,1)}, u32[]{:S(2)}) copy-start(bf16[64,64,128]{2,1,0:T(8,128)(2,1)} %fusion.187) | copy-start | bytes 3145732 | tf_op jit(solution)/shard_map/while
  420.4 9.7 copy-start.1
  432.3 11.2 %copy-start.2 = (bf16[64,64,128]{2,1,0:T(8,128)(2,1)S(1)}, bf16[64,64,128]{2,1,0:T(8,128)(2,1)}, u32[]{:S(2)}) copy-start(bf16[64,64,128]{2,1,0:T(8,128)(2,1)} %fusion.187) | copy-start | bytes 3145732 | tf_op jit(solution)/shard_map/while
  462.0 9.7 copy-start.1
  473.9 11.2 %copy-start.2 = (bf16[64,64,128]{2,1,0:T(8,128)(2,1)S(1)}, bf16[64,64,128]{2,1,0:T(8,128)(2,1)}, u32[]{:S(2)}) copy-start(bf16[64,64,128]{2,1,0:T(8,128)(2,1)} %fusion.187) | copy-start | bytes 3145732 | tf_op jit(solution)/shard_map/while
  503.6 9.7 copy-start.1
  515.5 11.2 %copy-start.2 = (bf16[64,64,128]{2,1,0:T(8,128)(2,1)S(1)}, bf16[64,64,128]{2,1,0:T(8,128)(2,1)}, u32[]{:S(2)}) copy-start(bf16[64,64,128]{2,1,0:T(8,128)(2,1)} %fusion.187) | copy-start | bytes 3145732 | tf_op jit(solution)/shard_map/while
  545.2 9.7 copy-start.1
  557.0 11.2 %copy-start.2 = (bf16[64,64,128]{2,1,0:T(8,128)(2,1)S(1)}, bf16[64,64,128]{2,1,0:T(8,128)(2,1)}, u32[]{:S(2)}) copy-start(bf16[64,64,128]{2,1,0:T(8,128)(2,1)} %fusion.187) | copy-start | bytes 3145732 | tf_op jit(solution)/shard_map/while
  598.6 11.2 %copy-start.2 = (bf16[64,64,128]{2,1,0:T(8,128)(2,1)S(1)}, bf16[64,64,128]{2,1,0:T(8,128)(2,1)}, u32[]{:S(2)}) copy-start(bf16[64,64,128]{2,1,0:T(8,128)(2,1)} %fusion.187) | copy-start | bytes 3145732 | tf_op jit(solution)/shard_map/while
  640.2 11.2 %copy-start.2 = (bf16[64,64,128]{2,1,0:T(8,128)(2,1)S(1)}, bf16[64,64,128]{2,1,0:T(8,128)(2,1)}, u32[]{:S(2)}) copy-start(bf16[64,64,128]{2,1,0:T(8,128)(2,1)} %fusion.187) | copy-start | bytes 3145732 | tf_op jit(solution)/shard_map/while
  681.7 11.2 %copy-start.2 = (bf16[64,64,128]{2,1,0:T(8,128)(2,1)S(1)}, bf16[64,64,128]{2,1,0:T(8,128)(2,1)}, u32[]{:S(2)}) copy-start(bf16[64,64,128]{2,1,0:T(8,128)(2,1)} %fusion.187) | copy-start | bytes 3145732 | tf_op jit(solution)/shard_map/while
  714.6 161.1 %all-reduce.10.cloned.1.call-start = ((), (), s32[]{:S(2)}) async-start(), calls=%async_computation.4 | async-start | bytes 8388608 | tf_op jit(solution)/shard_map/psum | solution.py:118
  727.2 288.3 %reduce-scatter.5.cloned.1.call-start = ((), (), s32[]{:S(2)}) async-start(), calls=%async_computation.6 | async-start | bytes 1081344 | tf_op jit(solution)/shard_map/reduce_scatter | solution.py:131
  (14 other events, 58.3 us)
Sparse Core Ops, SparseCore 0:
  159.5 36.9 all-reduce.5
  231.4 53.2 all-reduce.11
  343.0 33.6 all-reduce.7
  714.7 76.4 reduce-scatter.2
  794.3 81.3 all-reduce.9
  878.4 137.0 reduce-scatter.4
where the time goes:
time: 1040 us; the launch traced here: 1030 us
  matrix products  558 us (54%)
  waiting for transfers between devices  371 us (36%)
  other arithmetic  41.4 us (4%)
  local copies, waits for them, and re-layouts  40.3 us (4%)
  between operations  15.4 us (1%)
    reduce_scatter x1, waiting for transfers between devices, per_device(): lax.psum_scatter(jnp.einsum('kb,bde->kde', owners, outer, precision=highe...  140 us
    dot_general x2, matrix products, per_device(): row_slots = jnp.einsum('pij,pj->pi', kernel, tgt_picked, precision=highest)  112 us
    dot_general x8, matrix products, gradient_group(): jnp.einsum('gb,dgi->dbi', tgt_sel, dy_term, precision=highest)  89 us
    dot_general x8, matrix products, gradient_group(): jnp.einsum('gb,dgi->dbi', src_sel, dx_term, precision=highest)  88.5 us
    psum x1, waiting for transfers between devices, per_device(): tgt_grad = lax.psum(dy_total.reshape(feat_width, tgt_cells), 'src')  79.4 us
    dot_general x2, matrix products, per_device(): col_slots = jnp.einsum('pij,pi->pj', kernel, src_picked, precision=highest)  64.3 us
    reduce_scatter x1, waiting for transfers between devices, per_device(): lax.psum_scatter(dx_total, 'tgt', scatter_dimension=1, tiled=True)  61.7 us
    psum x1, waiting for transfers between devices, per_device(): col_sums = lax.psum(col_part, 'src')  53.3 us
  transfers between devices with their start and end apart: 6, of which 6 were waited for; matrix products, arithmetic and copies ran while one was open for 5% of the time, Pallas kernels for 0%

commit v1 on v0

v1 whole, which is shorter than its diff:
```python
import functools
import math

import jax
import jax.numpy as jnp
from jax import lax
from jax.experimental import pallas as pl
from jax.experimental.pallas import tpu as pltpu
from jax.sharding import PartitionSpec as P

BLK = 128
ENC_DEV = 1
ENTROPY = 0.5
POWER = 0.4
AUG = 16
UNROLL = 8
BF = jnp.bfloat16
F32 = jnp.float32
NT_DIMS = (((1,), (1,)), ((), ()))


def split3(value):
    high = value.astype(BF).astype(F32)
    rest = value - high
    mid = rest.astype(BF).astype(F32)
    return high, mid, rest - mid


def lanes(index):
    return pl.ds(pl.multiple_of(index * BLK, BLK), BLK)


def augment(norm_part, own_first):
    high, mid, low = split3(norm_part)
    row = lax.broadcasted_iota(jnp.int32, (AUG, BLK), 0)
    own = 0 if own_first else 3
    ones = 3 - own
    out = jnp.where((row >= ones) & (row < ones + 3), 1.0, 0.0).astype(F32)
    for place, term in enumerate((high, mid, low)):
        out = jnp.where(row == own + place, term, out)
    return out


def prepare(x_ref, y_ref, src_log, tgt_log, x_aug, y_aug, gain):
    feat = x_ref.shape[0]
    depth = x_aug.shape[1]
    src_blocks = x_ref.shape[1] // BLK
    tgt_blocks = y_ref.shape[1] // BLK

    def term(block, log_ref, index):
        norm = jnp.sum(jnp.square(block), axis=0, keepdims=True)
        value = -0.5 * norm
        if log_ref is not None:
            value = value + log_ref[pl.ds(index, 1), :] * (1.0 / gain)
        return value

    pad = jnp.zeros((depth - feat - AUG, BLK), F32)

    def src_one(index, _):
        block = x_ref[:, lanes(index)].astype(F32)
        full = jnp.concatenate([block, augment(term(block, src_log, index), True), pad], axis=0)
        x_aug[lanes(index), :] = full.T.astype(BF)
        return 0

    def tgt_one(index, _):
        bf_block = y_ref[:, lanes(index)]
        extra = augment(term(bf_block.astype(F32), tgt_log, index), False)
        y_aug[:feat, lanes(index)] = bf_block
        y_aug[feat:, lanes(index)] = jnp.concatenate([extra, pad], axis=0).astype(BF)
        return 0

    lax.fori_loop(0, src_blocks, src_one, 0, unroll=4)
    lax.fori_loop(0, tgt_blocks, tgt_one, 0, unroll=4)
    column = lax.broadcasted_iota(jnp.int32, (BLK, depth), 1)
    x_aug[pl.ds(src_blocks * BLK, BLK), :] = jnp.where(column == feat, -131072.0, 0.0).astype(BF)


def pair_of(code_ref, count, slot, src_blocks, tgt_blocks):
    code = code_ref[slot]
    shift = tgt_blocks.bit_length() - 1
    if tgt_blocks == 1 << shift:
        src_id, tgt_id = lax.shift_right_logical(code, shift), code & (tgt_blocks - 1)
    else:
        src_id, tgt_id = code // tgt_blocks, code % tgt_blocks
    return src_id, tgt_id, jnp.where(slot < count, src_id, src_blocks)


def plan_block(x_aug, y_aug, load_id, tgt_id, gain):
    acc = jnp.dot(x_aug[lanes(load_id), :], y_aug[:, lanes(tgt_id)], preferred_element_type=F32)
    return jnp.exp2(acc * (gain * math.log2(math.e)))


def split_wide(plan):
    high = plan.astype(BF)
    low = (plan - high.astype(F32)).astype(BF)
    return high, jnp.concatenate([high, low], axis=1)


def fold(plan):
    return jnp.sum(plan.reshape(BLK // 8, 8, BLK), axis=0)


def sums_kernel(first, gain, code_ref, count_ref, x_ref, y_ref, *refs):
    src_blocks = x_ref.shape[1] // BLK
    tgt_blocks = y_ref.shape[1] // BLK
    if first:
        row_out, col_out, x_aug, y_aug, row_acc, col_acc = refs
        src_log = tgt_log = None
    else:
        (growth, mass, row_in, col_in, row_out, col_out, src_log, tgt_log, x_aug, y_aug,
         row_acc, col_acc) = refs
        src_log[...] = POWER * (growth[...] - jnp.log(row_in[...]))
        tgt_log[...] = POWER * (jnp.log(mass[...]) - jnp.log(col_in[...]))
    prepare(x_ref, y_ref, src_log, tgt_log, x_aug, y_aug, gain)
    row_acc[...] = jnp.zeros_like(row_acc)
    col_acc[...] = jnp.zeros_like(col_acc)
    count = count_ref[0]
    pick = jnp.where(lax.broadcasted_iota(jnp.int32, (8, 2 * BLK), 0) == 0, 1.0, 0.0).astype(BF)

    def step(group, _):
        parts = []
        for inner in range(UNROLL):
            slot = group * UNROLL + inner
            src_id, tgt_id, load_id = pair_of(code_ref, count, slot, src_blocks, tgt_blocks)
            plan = plan_block(x_aug, y_aug, load_id, tgt_id, gain)
            _, wide = split_wide(plan)
            rows = lax.dot_general(pick, wide, NT_DIMS, preferred_element_type=F32)
            parts.append((src_id, tgt_id, rows, fold(plan)))
        for src_id, tgt_id, rows, cols in parts:
            row_acc[src_id] += rows
            col_acc[tgt_id] += cols
        return 0

    lax.fori_loop(0, (count + UNROLL - 1) // UNROLL, step, 0)
    row_out[...] = jnp.sum(row_acc[...], axis=1)
    col_out[...] = jnp.sum(col_acc[...], axis=1)


def grads_kernel(gain, code_ref, count_ref, batch_ref, x_ref, y_ref, hid_ref, growth, mass,
                 row_in, col_in, src_prev, tgt_prev, src_pot, tgt_pot, dy_ref, adp_ref,
                 src_log, tgt_log, x_aug, y_aug, dx_acc, col_acc):
    feat = x_ref.shape[0]
    src_blocks = x_ref.shape[1] // BLK
    tgt_blocks = y_ref.shape[1] // BLK
    src_new = (0.5 + POWER) * src_prev[...] + POWER * (growth[...] - jnp.log(row_in[...]))
    tgt_new = (0.5 + POWER) * tgt_prev[...] + POWER * (jnp.log(mass[...]) - jnp.log(col_in[...]))
    src_log[...] = src_new
    tgt_log[...] = tgt_new
    src_pot[...] = ENTROPY * src_new
    tgt_pot[...] = ENTROPY * tgt_new
    prepare(x_ref, y_ref, src_log, tgt_log, x_aug, y_aug, gain)
    dx_acc[...] = jnp.zeros_like(dx_acc)
    dy_ref[...] = jnp.zeros_like(dy_ref)
    col_acc[...] = jnp.zeros_like(col_acc)
    adp_ref[...] = jnp.zeros_like(adp_ref)
    count = count_ref[0]
    wide_rows = feat + AUG
    kept = feat + 8
    pick = jnp.where(
        lax.broadcasted_iota(jnp.int32, (wide_rows, BLK), 0) == feat, 1.0, 0.0
    ).astype(BF)
    group_size = UNROLL // 2

    def step(group, _):
        parts = []
        for inner in range(group_size):
            slot = group * group_size + inner
            src_id, tgt_id, load_id = pair_of(code_ref, count, slot, src_blocks, tgt_blocks)
            plan = plan_block(x_aug, y_aug, load_id, tgt_id, gain)
            high, wide = split_wide(plan)
            left = jnp.concatenate([y_aug[:wide_rows, lanes(tgt_id)], pick], axis=1)
            pulled = lax.dot_general(left, wide, NT_DIMS, preferred_element_type=F32)
            pushed = jnp.dot(x_ref[:, lanes(src_id)], high, preferred_element_type=F32)
            parts.append((src_id, tgt_id, pulled[:kept], pushed, fold(plan)))
        for src_id, tgt_id, pulled, pushed, cols in parts:
            dx_acc[src_id] += pulled
            dy_ref[:, lanes(tgt_id)] += pushed
            col_acc[tgt_id] += cols
        return 0

    lax.fori_loop(0, (count + group_size - 1) // group_size, step, 0)

    def finish_tgt(index, _):
        total = jnp.sum(col_acc[index], axis=0, keepdims=True)
        dy_ref[:, lanes(index)] = total * y_ref[:, lanes(index)].astype(F32) - dy_ref[:, lanes(index)]
        return 0

    lax.fori_loop(0, tgt_blocks, finish_tgt, 0, unroll=4)

    def finish_src(group, _):
        parts = []
        for inner in range(4):
            index = group * 4 + inner
            acc = dx_acc[index]
            grad = acc[feat:feat + 1] * x_ref[:, lanes(index)].astype(F32) - acc[:feat]
            _, wide = split_wide(grad)
            hid = hid_ref[:, lanes(index)]
            outer = lax.dot_general(
                jnp.concatenate([hid, hid], axis=1), wide, NT_DIMS, preferred_element_type=F32
            )
            parts.append((batch_ref[index], outer * (1.0 / BLK)))
        for batch, outer in parts:
            adp_ref[batch] += outer
        return 0

    lax.fori_loop(0, src_blocks // 4, finish_src, 0)


def local_calls(slots, feat, src_cells, tgt_cells, owners, interpret=False):
    src_blocks, tgt_blocks = src_cells // BLK, tgt_cells // BLK
    gain = 2.0 / (feat * ENTROPY)
    depth = -(-(feat + AUG) // BLK) * BLK
    smem = pl.BlockSpec(memory_space=pltpu.SMEM)
    vmem = pl.BlockSpec(memory_space=pltpu.VMEM)
    row_shape = jax.ShapeDtypeStruct((src_blocks, BLK), F32)
    col_shape = jax.ShapeDtypeStruct((tgt_blocks, BLK), F32)
    aug = [pltpu.VMEM((src_cells + BLK, depth), BF), pltpu.VMEM((depth, tgt_cells), BF)]
    col_acc = pltpu.VMEM((tgt_blocks, 8, BLK), F32)
    params = pltpu.CompilerParams(vmem_limit_bytes=56 * 1024 * 1024)

    def sums(first):
        scratch = aug + [pltpu.VMEM((src_blocks, 8, BLK), F32), col_acc]
        outs = [row_shape, col_shape] + ([] if first else [row_shape, col_shape])
        return pl.pallas_call(
            functools.partial(sums_kernel, first, gain),
            out_shape=outs,
            in_specs=[smem] * 2 + [vmem] * (2 if first else 6),
            out_specs=[vmem] * len(outs),
            scratch_shapes=scratch,
            compiler_params=params,
            interpret=interpret,
        )

    grads = pl.pallas_call(
        functools.partial(grads_kernel, gain),
        out_shape=[
            row_shape,
            col_shape,
            jax.ShapeDtypeStruct((feat, tgt_cells), F32),
            jax.ShapeDtypeStruct((owners, feat, feat), F32),
        ],
        in_specs=[smem] * 3 + [vmem] * 9,
        out_specs=[vmem] * 4,
        scratch_shapes=[pltpu.VMEM((src_blocks, BLK), F32), pltpu.VMEM((tgt_blocks, BLK), F32)]
        + aug
        + [pltpu.VMEM((src_blocks, feat + 8, BLK), F32), col_acc],
        compiler_params=params,
        interpret=interpret,
    )
    return sums(True), sums(False), grads


def per_device(src_emb, tgt_emb, src_hidden, growth, tgt_mass, pair_code, pair_count, block_batch):
    feat, src_cells = src_emb.shape
    tgt_cells = tgt_emb.shape[1]
    owners = ENC_DEV * lax.axis_size(("src", "tgt"))
    codes = pair_code.reshape(-1)
    count = pair_count.reshape(-1)
    first, later, grads = local_calls(codes.shape[0], feat, src_cells, tgt_cells, owners)
    growth = growth.reshape(-1, BLK)
    mass = tgt_mass.reshape(-1, BLK)
    row, col = first(codes, count, src_emb, tgt_emb)
    row, col = lax.psum(row, "tgt"), lax.psum(col, "src")
    row, col, src_log, tgt_log = later(codes, count, src_emb, tgt_emb, growth, mass, row, col)
    row, col = lax.psum(row, "tgt"), lax.psum(col, "src")
    src_pot, tgt_pot, dy, adapter = grads(
        codes, count, block_batch, src_emb, tgt_emb, src_hidden, growth, mass, row, col, src_log,
        tgt_log,
    )
    tgt_grad = lax.psum(dy, "src")
    adapter_grad = lax.psum_scatter(adapter, ("src", "tgt"), scatter_dimension=0, tiled=True)
    return src_pot.reshape(-1), tgt_pot.reshape(-1), tgt_grad, adapter_grad


def solution(mesh):
    in_specs = (
        P(None, "src"),
        P(None, "tgt"),
        P(None, "src"),
        P("src"),
        P("tgt"),
        P("src", "tgt", None),
        P("src", "tgt"),
        P("src"),
    )
    out_specs = (P("src"), P("tgt"), P(None, "tgt"), P(("src", "tgt"), None, None))
    return jax.shard_map(
        per_device, mesh=mesh, in_specs=in_specs, out_specs=out_specs, check_vma=False
    )
```

time: 1040 us -> 653 us (0.63); the launches traced: 1030 us -> 655 us
  matrix products: 558 us -> 0 us
  Pallas kernels: 0 us -> 139 us
  waiting for transfers between devices: 371 us -> 497 us
  other arithmetic: 41.4 us -> 0 us
  local copies, waits for them, and re-layouts: 40.3 us -> 4.5 us
    dot_general x118 -> x0, matrix products: 558 us -> none  [the longest x2 112 us: per_device(): row_slots = jnp.einsum('pij,pj->pi', kernel, tgt_picked, precision=highest)]
    psum x4 -> x5, waiting for transfers between devices: 169 us -> 310 us  [the longest x4 229 us: per_device(): row, col = (lax.psum(row, 'tgt'), lax.psum(col, 'src'))]
    pallas_call x0 -> x3, Pallas kernels: none -> 139 us  [the longest x1 68.1 us: per_device(): grads(codes, count, block_batch, src_emb, tgt_emb, src_hidden, growth, ma...]
    reduce_sum x10 -> x0, other arithmetic: 36.8 us -> none  [the longest x8 34 us: gradient_group(): jnp.sum(transport, axis=1)[None] * y_part.astype(jnp.float32) - pushed]
    while x50 -> x0, local copies, waits for them, and re-layouts: 20.3 us -> none  [the longest x2 11 us: per_device(): lax.scan(gradient_group, start_grads, (src_sel_groups, tgt_sel_groups, ke...]
    reduce_scatter x2 -> x1, waiting for transfers between devices: 201 us -> 184 us  [per_device(): lax.psum_scatter(adapter, ('src', 'tgt'), scatter_dimension=0, tiled=True)]
    unnamed x22 -> x1, local copies, waits for them, and re-layouts: 18.2 us -> 4.5 us
  transfers between devices with their start and end apart: 6 -> 6, of which waited for: 6 -> 6; matrix products, arithmetic and copies ran while one was open for 5% -> 0% of each run, Pallas kernels for 0% -> 0%
where the time goes in v1:
time: 653 us; the launch traced here: 655 us
  waiting for transfers between devices  497 us (76%)
  Pallas kernels  139 us (21%)
  between operations  14.8 us (2%)
    psum x4, waiting for transfers between devices, per_device(): row, col = (lax.psum(row, 'tgt'), lax.psum(col, 'src'))  229 us
    reduce_scatter x1, waiting for transfers between devices, per_device(): lax.psum_scatter(adapter, ('src', 'tgt'), scatter_dimension=0, tiled=True)  184 us
    psum x1, waiting for transfers between devices, per_device(): tgt_grad = lax.psum(dy, 'src')  81.3 us
    pallas_call x1, Pallas kernels, per_device(): grads(codes, count, block_batch, src_emb, tgt_emb, src_hidden, growth, ma...  68.1 us
    pallas_call x1, Pallas kernels, per_device(): later(codes, count, src_emb, tgt_emb, growth, mass, row, col)  35.3 us
    pallas_call x1, Pallas kernels, per_device(): row, col = first(codes, count, src_emb, tgt_emb)  35.1 us
  transfers between devices with their start and end apart: 6, of which 6 were waited for; matrix products, arithmetic and copies ran while one was open for 0% of the time, Pallas kernels for 0%

profile of v1, /device:TPU:0, one launch (start us, length us, event | category | flops | bytes accessed | tf_op | source)
XLA Modules:
  0.0 654.6 jit_solution(8580354345546986377)
XLA Ops:
  7.2 0.0 all-reduce.8.cloned.1.call-start
  7.9 35.1 %shard_map.111 = (f32[128,128]{1,0:T(8,128)}, f32[128,128]{1,0:T(8,128)}) custom-call(s32[512]{0:T(512)} %bitcast.13, s32[1]{0:T(128)} %bitcast.6.count_ref, bf16[64,16384]{1,0:T(8,128)(2,1)} %x_ref.5, bf16[64,16384]{1,0:T(8,128)(2,1)} %y_ref.5), custom_call_target="tpu_custom_call" | custom-call | tf_op jit(solution)/shard_map/pallas_call | solution.py:262
  43.0 0.0 all-reduce.8.cloned.1.call-update
  43.0 0.0 all-reduce.6.cloned.1.call-start
  43.1 0.7 all-reduce.6.cloned.1.call-update
  43.8 0.0 all-reduce.12.cloned.1.call-start
  43.8 79.7 %all-reduce.8.cloned.1.call-done.refs_3_ = f32[128,128]{1,0:T(8,128)} async-done(((f32[128,128]{1,0:T(8,128)}), f32[128,128]{1,0:T(8,128)}) %all-reduce.8.cloned.1.call-update) | async-done | bytes 65552 | tf_op jit(solution)/shard_map/psum | solution.py:263
  123.5 36.6 %all-reduce.6.cloned.1.call-done.refs_2_ = f32[128,128]{1,0:T(8,128)} async-done(((f32[128,128]{1,0:T(8,128)}), f32[128,128]{1,0:T(8,128)}) %all-reduce.6.cloned.1.call-update) | async-done | bytes 65552 | tf_op jit(solution)/shard_map/psum | solution.py:263
  160.2 35.3 %shard_map.112 = (f32[128,128]{1,0:T(8,128)}, f32[128,128]{1,0:T(8,128)}, f32[128,128]{1,0:T(8,128)}, f32[128,128]{1,0:T(8,128)}) custom-call(s32[512]{0:T(512)} %bitcast.14, s32[1]{0:T(128)} %bitcast.7.count_ref, bf16[64,16384]{1,0:T(8,128)(2,1)} %x_ref.5, bf16[64,16384]{1,0:T(8,128)(2,1)} %y_ref.5, f32[128,128]{1,0:T(8,128)} %bitcast.9, ...), custom_call_target="tpu_custom_call" | custom-call | tf_op jit(solution)/shard_map/pallas_call | solution.py:264
  195.5 0.0 all-reduce.12.cloned.1.call-update
  195.5 0.0 all-reduce.10.cloned.1.call-start
  195.6 0.5 all-reduce.10.cloned.1.call-update
  196.1 0.0 reduce-scatter.2.cloned.1.call-start
  196.1 76.3 %all-reduce.12.cloned.1.call-done.col_in = f32[128,128]{1,0:T(8,128)} async-done(((f32[128,128]{1,0:T(8,128)}), f32[128,128]{1,0:T(8,128)}) %all-reduce.12.cloned.1.call-update) | async-done | bytes 65552 | tf_op jit(solution)/shard_map/psum | solution.py:265
  272.5 36.5 %all-reduce.10.cloned.1.call-done.row_in = f32[128,128]{1,0:T(8,128)} async-done(((f32[128,128]{1,0:T(8,128)}), f32[128,128]{1,0:T(8,128)}) %all-reduce.10.cloned.1.call-update) | async-done | bytes 65552 | tf_op jit(solution)/shard_map/psum | solution.py:265
  308.9 68.1 %shard_map.113 = (f32[128,128]{1,0:T(8,128)}, f32[128,128]{1,0:T(8,128)}, f32[64,16384]{1,0:T(8,128)}, f32[32,64,64]{2,1,0:T(8,128)}) custom-call(s32[512]{0:T(512)} %bitcast.15, s32[1]{0:T(128)} %bitcast.8.count_ref, s32[128]{0:T(128)} %batch_ref.1, bf16[64,16384]{1,0:T(8,128)(2,1)} %x_ref.5, bf16[64,16384]{1,0:T(8,128)(2,1)} %y_ref.5, ...), custom_call_target="tpu_custom_call" | custom-call | tf_op jit(solution)/shard_map/pallas_call | solution.py:266
  377.0 0.0 reduce-scatter.2.cloned.1.call-update
  377.0 0.0 all-reduce.14.cloned.1.call-start
  377.1 0.5 all-reduce.14.cloned.1.call-update
  377.6 184.3 %reduce-scatter.2.cloned.1.call-done = f32[1,64,64]{2,1,0:T(8,128)} async-done(((f32[32,64,64]{2,1,0:T(8,128)}), f32[1,64,64]{2,1,0:T(8,128)}) %reduce-scatter.2.cloned.1.call-update) | async-done | bytes 16400 | tf_op jit(solution)/shard_map/reduce_scatter | solution.py:271
  561.9 81.3 %all-reduce.14.cloned.1.call-done = f32[64,16384]{1,0:T(8,128)} async-done(((f32[64,16384]{1,0:T(8,128)}), f32[64,16384]{1,0:T(8,128)}) %all-reduce.14.cloned.1.call-update) | async-done | bytes 4194320 | tf_op jit(solution)/shard_map/psum | solution.py:270
  643.2 4.5 copy.18
Async XLA Ops:
  7.2 116.4 %all-reduce.8.cloned.1.call-start = ((), (), s32[]{:S(2)}) async-start(), calls=%async_computation.2 | async-start | bytes 131072 | tf_op jit(solution)/shard_map/psum | solution.py:263
  43.0 117.2 %all-reduce.6.cloned.1.call-start = ((), (), s32[]{:S(2)}) async-start(), calls=%async_computation.1 | async-start | bytes 131072 | tf_op jit(solution)/shard_map/psum | solution.py:263
  43.8 228.7 %all-reduce.12.cloned.1.call-start = ((), (), s32[]{:S(2)}) async-start(), calls=%async_computation.4 | async-start | bytes 131072 | tf_op jit(solution)/shard_map/psum | solution.py:265
  195.5 113.4 %all-reduce.10.cloned.1.call-start = ((), (), s32[]{:S(2)}) async-start(), calls=%async_computation.3 | async-start | bytes 131072 | tf_op jit(solution)/shard_map/psum | solution.py:265
  196.1 365.8 %reduce-scatter.2.cloned.1.call-start = ((), (), s32[]{:S(2)}) async-start(), calls=%async_computation.6 | async-start | bytes 1081344 | tf_op jit(solution)/shard_map/reduce_scatter | solution.py:271
  377.0 266.2 %all-reduce.14.cloned.1.call-start = ((), (), s32[]{:S(2)}) async-start(), calls=%async_computation.5 | async-start | bytes 8388608 | tf_op jit(solution)/shard_map/psum | solution.py:270
Sparse Core Ops, SparseCore 0:
  43.1 80.3 all-reduce.7
  126.4 33.6 all-reduce.5
  195.6 76.7 all-reduce.11
  275.2 33.6 all-reduce.9
  377.1 184.6 reduce-scatter.1
  565.6 77.5 all-reduce.13

commit v2 on v1

--- a/solution.py
+++ b/solution.py
@@ -200,10 +200,207 @@
             )
             parts.append((batch_ref[index], outer * (1.0 / BLK)))
         for batch, outer in parts:
-            adp_ref[batch] += outer
+            adp_ref[batch] += jnp.concatenate([outer[:feat // 2], outer[feat // 2:]], axis=1)
         return 0
 
     lax.fori_loop(0, src_blocks // 4, finish_src, 0)
+
+
+def flip(position, bit):
+    size = 1 << bit
+    return position + size * (1 - 2 * ((position // size) % 2))
+
+
+def greet(partners):
+    barrier = pltpu.get_barrier_semaphore()
+    for partner in partners:
+        pl.semaphore_signal(barrier, inc=1, device_id=partner, device_id_type=pl.DeviceIdType.MESH)
+    pl.semaphore_wait(barrier, len(partners))
+
+
+def send(source, target, sems, slot, partner):
+    copy = pltpu.make_async_remote_copy(
+        src_ref=source,
+        dst_ref=target,
+        send_sem=sems.at[0, slot],
+        recv_sem=sems.at[1, slot],
+        device_id=partner,
+        device_id_type=pl.DeviceIdType.MESH,
+    )
+    copy.start()
+    return copy
+
+
+def small_sums_kernel(sizes, row_in, col_in, row_out, col_out, row_got, col_got, *sems):
+    axes = (
+        ("tgt", row_in, row_out, row_got, sems[0], sems[1]),
+        ("src", col_in, col_out, col_got, sems[2], sems[3]),
+    )
+    places = {axis: lax.axis_index(axis) for axis in sizes}
+    greet([{axis: lax.rem(places[axis] + step, sizes[axis])} for axis in sizes
+           for step in range(1, sizes[axis])])
+
+    def share(ref, axis, owner):
+        rows = ref.shape[0] // sizes[axis]
+        return ref.at[pl.ds(pl.multiple_of(owner * rows, rows), rows)]
+
+    copies = {}
+    for axis, source, _, got, first, _ in axes:
+        copies[axis] = []
+        for step in range(1, sizes[axis]):
+            peer = lax.rem(places[axis] + step, sizes[axis])
+            copies[axis].append(
+                send(share(source, axis, peer), got.at[step], first, step, {axis: peer})
+            )
+    for axis, source, out, got, _, second in axes:
+        for copy in copies[axis]:
+            copy.wait()
+        total = share(source, axis, places[axis])[...]
+        for step in range(1, sizes[axis]):
+            total = total + got[step]
+        share(out, axis, places[axis])[...] = total
+        copies[axis] = []
+        for step in range(1, sizes[axis]):
+            peer = lax.rem(places[axis] + step, sizes[axis])
+            mine = share(out, axis, places[axis])
+            copies[axis].append(send(mine, mine, second, step, {axis: peer}))
+    for axis in sizes:
+        for copy in copies[axis]:
+            copy.wait()
+
+
+def small_sums(sizes, row, col):
+    vmem = pl.BlockSpec(memory_space=pltpu.VMEM)
+    scratch = []
+    for axis, part in (("tgt", row), ("src", col)):
+        scratch.append(pltpu.VMEM((sizes[axis], part.shape[0] // sizes[axis], BLK), F32))
+    for axis in ("tgt", "src"):
+        scratch += [pltpu.SemaphoreType.DMA((2, sizes[axis]))] * 2
+    return pl.pallas_call(
+        functools.partial(small_sums_kernel, sizes),
+        out_shape=[jax.ShapeDtypeStruct(part.shape, F32) for part in (row, col)],
+        in_specs=[vmem] * 2,
+        out_specs=[vmem] * 2,
+        scratch_shapes=scratch,
+        compiler_params=pltpu.CompilerParams(collective_id=0, has_side_effects=True),
+    )(row, col)
+
+
+def columns(ref, start, size):
+    return ref.at[:, pl.ds(pl.multiple_of(start, BLK), size)]
+
+
+def add_columns(out, out_at, left, left_at, right, size):
+    chunk = min(size, 8 * BLK)
+
+    def one(index, _):
+        shift = index * chunk
+        columns(out, out_at + shift, chunk)[...] = (
+            columns(left, left_at + shift, chunk)[...] + columns(right, shift, chunk)[...]
+        )
+        return 0
+
+    lax.fori_loop(0, size // chunk, one, 0)
+
+
+def last_sums_kernel(sizes, dy_in, adp_in, dy_out, adp_out, adp_sum, adp_got, *refs):
+    bits = sizes["src"].bit_length() - 1
+    got = (refs[:bits], refs[bits:2 * bits])
+    adp_recv = refs[2 * bits:3 * bits]
+    dy_sems, adp_sems, end_sems = refs[3 * bits:]
+    me, mine_tgt = lax.axis_index("src"), lax.axis_index("tgt")
+    tgt_peers = [lax.rem(mine_tgt + step, sizes["tgt"]) for step in range(1, sizes["tgt"])]
+    greet([{"src": flip(me, bit)} for bit in range(bits)] + [{"tgt": peer} for peer in tgt_peers])
+    half = dy_in.shape[1] // 2
+    orders = (list(range(bits)), [0] + list(range(bits - 1, 0, -1)))
+    starts = [0, half]
+    sizes_now = half
+    mats_start, mats = 0, adp_in.shape[0]
+    history = []
+    for step in range(bits):
+        sizes_now //= 2
+        mats //= 2
+        copies, keeps, held = [], [], []
+        for stream in range(2):
+            bit = orders[stream][step]
+            side = (me // (1 << bit)) % 2
+            keep = starts[stream] + side * sizes_now
+            source = dy_in if step == 0 else got[stream][step - 1]
+            base = stream * half if step == 0 else 0
+            copies.append(send(columns(source, base + (1 - side) * sizes_now, sizes_now),
+                               got[stream][step], dy_sems, 2 * step + stream,
+                               {"src": flip(me, bit)}))
+            held.append((source, base + side * sizes_now))
+            keeps.append(keep)
+        side = (me // (1 << step)) % 2
+        source = adp_in if step == 0 else adp_sum
+        mats_give = mats_start + (1 - side) * mats
+        mats_start = mats_start + side * mats
+        copies.append(send(source.at[pl.ds(mats_give, mats)], adp_recv[step], adp_sems, step,
+                           {"src": flip(me, step)}))
+        for stream in range(2):
+            copies[stream].wait()
+            out, out_at = (got[stream][step], 0) if step < bits - 1 else (dy_out, keeps[stream])
+            add_columns(out, out_at, *held[stream], got[stream][step], sizes_now)
+        copies[2].wait()
+
+        def add_mat(index, _, source=source, mats_start=mats_start, step=step):
+            adp_sum[mats_start + index] = source[mats_start + index] + adp_recv[step][index]
+            return 0
+
+        lax.fori_loop(0, mats, add_mat, 0)
+        history.append((keeps, sizes_now))
+        starts = keeps
+    ends = []
+    for step, peer in enumerate(tgt_peers):
+        ends.append(send(adp_sum.at[mats_start + peer], adp_got.at[step], end_sems, step,
+                         {"tgt": peer}))
+    for step in range(bits - 1, -1, -1):
+        keeps, size = history[step]
+        copies = []
+        for stream in range(2):
+            area = columns(dy_out, keeps[stream], size)
+            copies.append(send(area, area, dy_sems, 2 * (bits + step) + stream,
+                               {"src": flip(me, orders[stream][step])}))
+        for copy in copies:
+            copy.wait()
+    total = adp_sum[mats_start + mine_tgt]
+    for step, copy in enumerate(ends):
+        copy.wait()
+        total = total + adp_got[step]
+    adp_out[...] = total
+
+
+def last_sums(sizes, dy, adapter):
+    bits = sizes["src"].bit_length() - 1
+    vmem = pl.BlockSpec(memory_space=pltpu.VMEM)
+    feat, cells = dy.shape
+    owners, mat_rows, mat_cols = adapter.shape
+    parts = [pltpu.VMEM((feat, cells >> (step + 2)), F32) for step in range(bits)]
+    mats = [pltpu.VMEM((owners >> (step + 1), mat_rows, mat_cols), F32) for step in range(bits)]
+    return pl.pallas_call(
+        functools.partial(last_sums_kernel, sizes),
+        out_shape=[
+            jax.ShapeDtypeStruct(dy.shape, F32),
+            jax.ShapeDtypeStruct((mat_rows, mat_cols), F32),
+        ],
+        in_specs=[vmem] * 2,
+        out_specs=[vmem] * 2,
+        scratch_shapes=[
+            pltpu.VMEM(adapter.shape, F32),
+            pltpu.VMEM((max(sizes["tgt"] - 1, 1), mat_rows, mat_cols), F32),
+        ]
+        + parts * 2
+        + mats
+        + [
+            pltpu.SemaphoreType.DMA((2, 4 * bits)),
+            pltpu.SemaphoreType.DMA((2, bits)),
+            pltpu.SemaphoreType.DMA((2, max(sizes["tgt"] - 1, 1))),
+        ],
+        compiler_params=pltpu.CompilerParams(
+            collective_id=1, has_side_effects=True, vmem_limit_bytes=40 * 1024 * 1024
+        ),
+    )(dy, adapter)
 
 
 def local_calls(slots, feat, src_cells, tgt_cells, owners, interpret=False):
@@ -237,7 +434,7 @@
             row_shape,
             col_shape,
             jax.ShapeDtypeStruct((feat, tgt_cells), F32),
-            jax.ShapeDtypeStruct((owners, feat, feat), F32),
+            jax.ShapeDtypeStruct((owners, feat // 2, 2 * feat), F32),
         ],
         in_specs=[smem] * 3 + [vmem] * 9,
         out_specs=[vmem] * 4,
@@ -259,16 +456,20 @@
     first, later, grads = local_calls(codes.shape[0], feat, src_cells, tgt_cells, owners)
     growth = growth.reshape(-1, BLK)
     mass = tgt_mass.reshape(-1, BLK)
-    row, col = first(codes, count, src_emb, tgt_emb)
-    row, col = lax.psum(row, "tgt"), lax.psum(col, "src")
+    sizes = {axis: lax.axis_size(axis) for axis in ("src", "tgt")}
+    bits = sizes["src"].bit_length() - 1
+    owner_src = block_batch // sizes["tgt"]
+    spot = sum((owner_src // (1 << bit)) % 2 * (1 << (bits - 1 - bit)) for bit in range(bits))
+    spots = spot * sizes["tgt"] + block_batch % sizes["tgt"]
+    row, col = small_sums(sizes, *first(codes, count, src_emb, tgt_emb))
     row, col, src_log, tgt_log = later(codes, count, src_emb, tgt_emb, growth, mass, row, col)
-    row, col = lax.psum(row, "tgt"), lax.psum(col, "src")
+    row, col = small_sums(sizes, row, col)
     src_pot, tgt_pot, dy, adapter = grads(
-        codes, count, block_batch, src_emb, tgt_emb, src_hidden, growth, mass, row, col, src_log,
+        codes, count, spots, src_emb, tgt_emb, src_hidden, growth, mass, row, col, src_log,
         tgt_log,
     )
-    tgt_grad = lax.psum(dy, "src")
-    adapter_grad = lax.psum_scatter(adapter, ("src", "tgt"), scatter_dimension=0, tiled=True)
+    tgt_grad, packed = last_sums(sizes, dy, adapter)
+    adapter_grad = jnp.concatenate([packed[:, :feat], packed[:, feat:]], axis=0)[None]
     return src_pot.reshape(-1), tgt_pot.reshape(-1), tgt_grad, adapter_grad
 
 

time: 653 us -> 333 us (0.51)
  waiting for transfers between devices: 497 us -> 0 us
  Pallas kernels: 139 us -> 326 us
  between operations: 14.8 us -> 1.31 us
    psum x5 -> x0, waiting for transfers between devices: 310 us -> none  [the longest x4 229 us: per_device(): row, col = (lax.psum(row, 'tgt'), lax.psum(col, 'src'))]
    pallas_call x2 -> x5, Pallas kernels: 103 us -> 302 us  [the longest x1 128 us: last_sums(): pl.pallas_call(functools.partial(last_sums_kernel, sizes), out_shape=[jax...]
    reduce_scatter x1 -> x0, waiting for transfers between devices: 184 us -> none  [per_device(): lax.psum_scatter(adapter, ('src', 'tgt'), scatter_dimension=0, tiled=True)]
    pallas_call x1, Pallas kernels: 35.3 us -> 23.5 us  [per_device(): later(codes, count, src_emb, tgt_emb, growth, mass, row, col)]
  transfers between devices with their start and end apart: 6 -> 0, of which waited for: 6 -> 0; matrix products, arithmetic and copies ran while one was open for 0% -> 0% of each run, Pallas kernels for 0% -> 0%
where the time goes in v2:
time: 333 us; the launch traced here: 334 us
  Pallas kernels  326 us (98%)
  local copies, waits for them, and re-layouts  5.31 us (2%)
    pallas_call x1, Pallas kernels, last_sums(): pl.pallas_call(functools.partial(last_sums_kernel, sizes), out_shape=[jax...  128 us
    pallas_call x2, Pallas kernels, small_sums(): pl.pallas_call(functools.partial(small_sums_kernel, sizes), out_shape=[ja...  103 us
    pallas_call x1, Pallas kernels, per_device(): grads(codes, count, spots, src_emb, tgt_emb, src_hidden, growth, mass, ro...  47.9 us
    pallas_call x1, Pallas kernels, per_device(): later(codes, count, src_emb, tgt_emb, growth, mass, row, col)  23.5 us
    pallas_call x1, Pallas kernels, per_device(): row, col = small_sums(sizes, *first(codes, count, src_emb, tgt_emb))  23.2 us

profile of v2, /device:TPU:0, one launch (start us, length us, event | category | flops | bytes accessed | tf_op | source)
XLA Modules:
  0.0 334.3 jit_solution(11408865512607539326)
XLA Ops:
  1.3 1.3 fusion.1.batch_ref
  2.5 23.2 %shard_map.111 = (f32[128,128]{1,0:T(8,128)}, f32[128,128]{1,0:T(8,128)}) custom-call(s32[512]{0:T(512)} %bitcast.15, s32[1]{0:T(128)} %bitcast.8.count_ref, bf16[64,16384]{1,0:T(8,128)(2,1)} %x_ref.5, bf16[64,16384]{1,0:T(8,128)(2,1)} %y_ref.5), custom_call_target="tpu_custom_call" | custom-call | tf_op jit(solution)/shard_map/pallas_call | solution.py:464
  25.8 52.5 %shard_map.112 = (f32[128,128]{1,0:T(8,128)}, f32[128,128]{1,0:T(8,128)}) custom-call(f32[128,128]{1,0:T(8,128)} %get-tuple-element.20.row_in, f32[128,128]{1,0:T(8,128)} %get-tuple-element.21.col_in), custom_call_target="tpu_custom_call" | custom-call | tf_op jit(solution)/shard_map/pallas_call | solution.py:279
  78.3 23.5 %shard_map.113 = (f32[128,128]{1,0:T(8,128)}, f32[128,128]{1,0:T(8,128)}, f32[128,128]{1,0:T(8,128)}, f32[128,128]{1,0:T(8,128)}) custom-call(s32[512]{0:T(512)} %bitcast.16, s32[1]{0:T(128)} %bitcast.9.count_ref, bf16[64,16384]{1,0:T(8,128)(2,1)} %x_ref.5, bf16[64,16384]{1,0:T(8,128)(2,1)} %y_ref.5, f32[128,128]{1,0:T(8,128)} %bitcast.11, ...), custom_call_target="tpu_custom_call" | custom-call | tf_op jit(solution)/shard_map/pallas_call | solution.py:465
  101.7 50.5 %shard_map.114 = (f32[128,128]{1,0:T(8,128)}, f32[128,128]{1,0:T(8,128)}) custom-call(f32[128,128]{1,0:T(8,128)} %get-tuple-element.24.row_in, f32[128,128]{1,0:T(8,128)} %get-tuple-element.25.col_in), custom_call_target="tpu_custom_call" | custom-call | tf_op jit(solution)/shard_map/pallas_call | solution.py:279
  152.3 47.9 %shard_map.115 = (f32[128,128]{1,0:T(8,128)}, f32[128,128]{1,0:T(8,128)}, f32[64,16384]{1,0:T(8,128)}, f32[32,32,128]{2,1,0:T(8,128)}) custom-call(s32[512]{0:T(512)} %bitcast.17, s32[1]{0:T(128)} %bitcast.10.count_ref, s32[128]{0:T(128)} %fusion.1.batch_ref, bf16[64,16384]{1,0:T(8,128)(2,1)} %x_ref.5, bf16[64,16384]{1,0:T(8,128)(2,1)} %y_ref.5, ...), custom_call_target="tpu_custom_call" | custom-call | tf_op jit(solution)/shard_map/pallas_call | solution.py:467
  200.2 0.0 copy-start
  200.2 2.2 copy-done
  202.3 0.0 copy-start.1
  202.3 1.0 copy-done.1
  203.4 128.2 %shard_map.116 = (f32[64,16384]{1,0:T(8,128)S(1)}, f32[32,128]{1,0:T(8,128)S(1)}) custom-call(f32[64,16384]{1,0:T(8,128)S(1)} %copy-done, f32[32,32,128]{2,1,0:T(8,128)S(1)} %copy-done.1), custom_call_target="tpu_custom_call" | custom-call | tf_op jit(solution)/shard_map/pallas_call | solution.py:381
  331.6 0.1 fusion.7
  331.7 0.6 maximum_bitcast_fusion
  332.3 2.0 copy.14
Async XLA Ops:
  200.2 2.2 copy-start
  202.3 1.0 copy-start.1

commit v3 on v2

--- a/solution.py
+++ b/solution.py
@@ -13,10 +13,9 @@
 ENTROPY = 0.5
 POWER = 0.4
 AUG = 16
-UNROLL = 8
+UNROLL = 16
 BF = jnp.bfloat16
 F32 = jnp.float32
-NT_DIMS = (((1,), (1,)), ((), ()))
 
 
 def split3(value):
@@ -41,7 +40,7 @@
     return out
 
 
-def prepare(x_ref, y_ref, src_log, tgt_log, x_aug, y_aug, gain):
+def prepare(x_ref, y_ref, src_log, tgt_log, x_aug, y_aug, gain, y_turned=None):
     feat = x_ref.shape[0]
     depth = x_aug.shape[1]
     src_blocks = x_ref.shape[1] // BLK
@@ -67,10 +66,13 @@
         extra = augment(term(bf_block.astype(F32), tgt_log, index), False)
         y_aug[:feat, lanes(index)] = bf_block
         y_aug[feat:, lanes(index)] = jnp.concatenate([extra, pad], axis=0).astype(BF)
-        return 0
-
-    lax.fori_loop(0, src_blocks, src_one, 0, unroll=4)
-    lax.fori_loop(0, tgt_blocks, tgt_one, 0, unroll=4)
+        if y_turned is not None:
+            full = jnp.concatenate([bf_block.astype(F32), extra, pad], axis=0)
+            y_turned[lanes(index), :] = full.T.astype(BF)
+        return 0
+
+    lax.fori_loop(0, src_blocks, src_one, 0, unroll=8)
+    lax.fori_loop(0, tgt_blocks, tgt_one, 0, unroll=8)
     column = lax.broadcasted_iota(jnp.int32, (BLK, depth), 1)
     x_aug[pl.ds(src_blocks * BLK, BLK), :] = jnp.where(column == feat, -131072.0, 0.0).astype(BF)
 
@@ -88,12 +90,6 @@
 def plan_block(x_aug, y_aug, load_id, tgt_id, gain):
     acc = jnp.dot(x_aug[lanes(load_id), :], y_aug[:, lanes(tgt_id)], preferred_element_type=F32)
     return jnp.exp2(acc * (gain * math.log2(math.e)))
-
-
-def split_wide(plan):
-    high = plan.astype(BF)
-    low = (plan - high.astype(F32)).astype(BF)
-    return high, jnp.concatenate([high, low], axis=1)
 
 
 def fold(plan):
@@ -115,30 +111,36 @@
     row_acc[...] = jnp.zeros_like(row_acc)
     col_acc[...] = jnp.zeros_like(col_acc)
     count = count_ref[0]
-    pick = jnp.where(lax.broadcasted_iota(jnp.int32, (8, 2 * BLK), 0) == 0, 1.0, 0.0).astype(BF)
-
     def step(group, _):
         parts = []
         for inner in range(UNROLL):
             slot = group * UNROLL + inner
             src_id, tgt_id, load_id = pair_of(code_ref, count, slot, src_blocks, tgt_blocks)
             plan = plan_block(x_aug, y_aug, load_id, tgt_id, gain)
-            _, wide = split_wide(plan)
-            rows = lax.dot_general(pick, wide, NT_DIMS, preferred_element_type=F32)
-            parts.append((src_id, tgt_id, rows, fold(plan)))
+            parts.append((src_id, tgt_id, jnp.sum(plan, axis=1, keepdims=True), fold(plan)))
         for src_id, tgt_id, rows, cols in parts:
-            row_acc[src_id] += rows
+            row_acc[src_id] = row_acc[src_id] + rows
             col_acc[tgt_id] += cols
         return 0
 
     lax.fori_loop(0, (count + UNROLL - 1) // UNROLL, step, 0)
-    row_out[...] = jnp.sum(row_acc[...], axis=1)
+    diagonal = lax.broadcasted_iota(jnp.int32, (BLK, BLK), 0) == lax.broadcasted_iota(
+        jnp.int32, (BLK, BLK), 1
+    )
+
+    def lay_flat(index, _):
+        row_out[pl.ds(index, 1), :] = jnp.sum(
+            jnp.where(diagonal, row_acc[index], 0.0), axis=0, keepdims=True
+        )
+        return 0
+
+    lax.fori_loop(0, src_blocks, lay_flat, 0, unroll=8)
     col_out[...] = jnp.sum(col_acc[...], axis=1)
 
 
 def grads_kernel(gain, code_ref, count_ref, batch_ref, x_ref, y_ref, hid_ref, growth, mass,
                  row_in, col_in, src_prev, tgt_prev, src_pot, tgt_pot, dy_ref, adp_ref,
-                 src_log, tgt_log, x_aug, y_aug, dx_acc, col_acc):
+                 src_log, tgt_log, x_aug, y_aug, y_turned, dx_acc, col_acc):
     feat = x_ref.shape[0]
     src_blocks = x_ref.shape[1] // BLK
     tgt_blocks = y_ref.shape[1] // BLK
@@ -148,17 +150,13 @@
     tgt_log[...] = tgt_new
     src_pot[...] = ENTROPY * src_new
     tgt_pot[...] = ENTROPY * tgt_new
-    prepare(x_ref, y_ref, src_log, tgt_log, x_aug, y_aug, gain)
+    prepare(x_ref, y_ref, src_log, tgt_log, x_aug, y_aug, gain, y_turned)
     dx_acc[...] = jnp.zeros_like(dx_acc)
     dy_ref[...] = jnp.zeros_like(dy_ref)
     col_acc[...] = jnp.zeros_like(col_acc)
     adp_ref[...] = jnp.zeros_like(adp_ref)
     count = count_ref[0]
-    wide_rows = feat + AUG
-    kept = feat + 8
-    pick = jnp.where(
-        lax.broadcasted_iota(jnp.int32, (wide_rows, BLK), 0) == feat, 1.0, 0.0
-    ).astype(BF)
+    is_sum = lax.broadcasted_iota(jnp.int32, (BLK, x_aug.shape[1]), 1) == feat
     group_size = UNROLL // 2
 
     def step(group, _):
@@ -167,15 +165,15 @@
             slot = group * group_size + inner
             src_id, tgt_id, load_id = pair_of(code_ref, count, slot, src_blocks, tgt_blocks)
             plan = plan_block(x_aug, y_aug, load_id, tgt_id, gain)
-            high, wide = split_wide(plan)
-            left = jnp.concatenate([y_aug[:wide_rows, lanes(tgt_id)], pick], axis=1)
-            pulled = lax.dot_general(left, wide, NT_DIMS, preferred_element_type=F32)
-            pushed = jnp.dot(x_ref[:, lanes(src_id)], high, preferred_element_type=F32)
-            parts.append((src_id, tgt_id, pulled[:kept], pushed, fold(plan)))
-        for src_id, tgt_id, pulled, pushed, cols in parts:
-            dx_acc[src_id] += pulled
-            dy_ref[:, lanes(tgt_id)] += pushed
-            col_acc[tgt_id] += cols
+            parts.append((src_id, tgt_id, plan.astype(BF), jnp.sum(plan, axis=1, keepdims=True)))
+            col_acc[tgt_id] += fold(plan)
+        for src_id, tgt_id, high, rows in parts:
+            pulled = jnp.dot(high, y_turned[lanes(tgt_id), :], preferred_element_type=F32)
+            dx_acc[src_id] += jnp.where(is_sum, rows, pulled)
+        for src_id, tgt_id, high, rows in parts:
+            dy_ref[:, lanes(tgt_id)] += jnp.dot(
+                x_ref[:, lanes(src_id)], high, preferred_element_type=F32
+            )
         return 0
 
     lax.fori_loop(0, (count + group_size - 1) // group_size, step, 0)
@@ -185,18 +183,20 @@
         dy_ref[:, lanes(index)] = total * y_ref[:, lanes(index)].astype(F32) - dy_ref[:, lanes(index)]
         return 0
 
-    lax.fori_loop(0, tgt_blocks, finish_tgt, 0, unroll=4)
+    lax.fori_loop(0, tgt_blocks, finish_tgt, 0, unroll=8)
 
     def finish_src(group, _):
         parts = []
         for inner in range(4):
             index = group * 4 + inner
             acc = dx_acc[index]
-            grad = acc[feat:feat + 1] * x_ref[:, lanes(index)].astype(F32) - acc[:feat]
-            _, wide = split_wide(grad)
+            turned = x_aug[lanes(index), :].astype(F32)
+            grad = (acc[:, feat:feat + 1] * turned - acc)[:, :feat]
+            high = grad.astype(BF)
+            both = jnp.concatenate([high, (grad - high.astype(F32)).astype(BF)], axis=0)
             hid = hid_ref[:, lanes(index)]
-            outer = lax.dot_general(
-                jnp.concatenate([hid, hid], axis=1), wide, NT_DIMS, preferred_element_type=F32
+            outer = jnp.dot(
+                jnp.concatenate([hid, hid], axis=1), both, preferred_element_type=F32
             )
             parts.append((batch_ref[index], outer * (1.0 / BLK)))
         for batch, outer in parts:
@@ -416,7 +416,7 @@
     params = pltpu.CompilerParams(vmem_limit_bytes=56 * 1024 * 1024)
 
     def sums(first):
-        scratch = aug + [pltpu.VMEM((src_blocks, 8, BLK), F32), col_acc]
+        scratch = aug + [pltpu.VMEM((src_blocks, BLK, BLK), F32), col_acc]
         outs = [row_shape, col_shape] + ([] if first else [row_shape, col_shape])
         return pl.pallas_call(
             functools.partial(sums_kernel, first, gain),
@@ -440,7 +440,11 @@
         out_specs=[vmem] * 4,
         scratch_shapes=[pltpu.VMEM((src_blocks, BLK), F32), pltpu.VMEM((tgt_blocks, BLK), F32)]
         + aug
-        + [pltpu.VMEM((src_blocks, feat + 8, BLK), F32), col_acc],
+        + [
+            pltpu.VMEM((tgt_cells, depth), BF),
+            pltpu.VMEM((src_blocks, BLK, depth), F32),
+            col_acc,
+        ],
         compiler_params=params,
         interpret=interpret,
     )

time: 333 us -> 186 us (0.56)
  Pallas kernels: 326 us -> 178 us
    pallas_call x2, Pallas kernels: 103 us -> 43.6 us  [small_sums(): pl.pallas_call(functools.partial(small_sums_kernel, sizes), out_shape=[ja...]
    pallas_call x1, Pallas kernels: 128 us -> 69.8 us  [last_sums(): pl.pallas_call(functools.partial(last_sums_kernel, sizes), out_shape=[jax...]
    pallas_call x1, Pallas kernels: 47.9 us -> 34.4 us  [per_device(): grads(codes, count, spots, src_emb, tgt_emb, src_hidden, growth, mass, ro...]
    pallas_call x1, Pallas kernels: 23.2 us -> 14.9 us  [per_device(): row, col = small_sums(sizes, *first(codes, count, src_emb, tgt_emb))]
    pallas_call x1, Pallas kernels: 23.5 us -> 15.1 us  [per_device(): later(codes, count, src_emb, tgt_emb, growth, mass, row, col)]
where the time goes in v3:
time: 186 us
  Pallas kernels  178 us (96%)
  local copies, waits for them, and re-layouts  5.31 us (3%)
  other arithmetic  1.88 us (1%)
    pallas_call x1, Pallas kernels, last_sums(): pl.pallas_call(functools.partial(last_sums_kernel, sizes), out_shape=[jax...  69.8 us
    pallas_call x2, Pallas kernels, small_sums(): pl.pallas_call(functools.partial(small_sums_kernel, sizes), out_shape=[ja...  43.6 us
    pallas_call x1, Pallas kernels, per_device(): grads(codes, count, spots, src_emb, tgt_emb, src_hidden, growth, mass, ro...  34.4 us
    pallas_call x1, Pallas kernels, per_device(): later(codes, count, src_emb, tgt_emb, growth, mass, row, col)  15.1 us
    pallas_call x1, Pallas kernels, per_device(): row, col = small_sums(sizes, *first(codes, count, src_emb, tgt_emb))  14.9 us
    unnamed x5, local copies, waits for them, and re-layouts  5.24 us

profile of v3, /device:TPU:0, one launch (start us, length us, event | category | flops | bytes accessed | tf_op | source)
XLA Modules:
  0.0 186.3 jit_solution(11481904807551978162)
XLA Ops:
  1.3 1.3 fusion.1.batch_ref
  2.5 14.9 %shard_map.111 = (f32[128,128]{1,0:T(8,128)}, f32[128,128]{1,0:T(8,128)}) custom-call(s32[512]{0:T(512)} %bitcast.15, s32[1]{0:T(128)} %bitcast.8.count_ref, bf16[64,16384]{1,0:T(8,128)(2,1)} %x_ref.5, bf16[64,16384]{1,0:T(8,128)(2,1)} %y_ref.5), custom_call_target="tpu_custom_call" | custom-call | tf_op jit(solution)/shard_map/pallas_call | solution.py:468
  17.4 23.9 %shard_map.112 = (f32[128,128]{1,0:T(8,128)}, f32[128,128]{1,0:T(8,128)}) custom-call(f32[128,128]{1,0:T(8,128)} %get-tuple-element.20.row_in, f32[128,128]{1,0:T(8,128)} %get-tuple-element.21.col_in), custom_call_target="tpu_custom_call" | custom-call | tf_op jit(solution)/shard_map/pallas_call | solution.py:279
  41.3 15.1 %shard_map.113 = (f32[128,128]{1,0:T(8,128)}, f32[128,128]{1,0:T(8,128)}, f32[128,128]{1,0:T(8,128)}, f32[128,128]{1,0:T(8,128)}) custom-call(s32[512]{0:T(512)} %bitcast.16, s32[1]{0:T(128)} %bitcast.9.count_ref, bf16[64,16384]{1,0:T(8,128)(2,1)} %x_ref.5, bf16[64,16384]{1,0:T(8,128)(2,1)} %y_ref.5, f32[128,128]{1,0:T(8,128)} %bitcast.11, ...), custom_call_target="tpu_custom_call" | custom-call | tf_op jit(solution)/shard_map/pallas_call | solution.py:469
  56.4 19.7 %shard_map.114 = (f32[128,128]{1,0:T(8,128)}, f32[128,128]{1,0:T(8,128)}) custom-call(f32[128,128]{1,0:T(8,128)} %get-tuple-element.24.row_in, f32[128,128]{1,0:T(8,128)} %get-tuple-element.25.col_in), custom_call_target="tpu_custom_call" | custom-call | tf_op jit(solution)/shard_map/pallas_call | solution.py:279
  76.2 34.4 %shard_map.115 = (f32[128,128]{1,0:T(8,128)}, f32[128,128]{1,0:T(8,128)}, f32[64,16384]{1,0:T(8,128)}, f32[32,32,128]{2,1,0:T(8,128)}) custom-call(s32[512]{0:T(512)} %bitcast.17, s32[1]{0:T(128)} %bitcast.10.count_ref, s32[128]{0:T(128)} %fusion.1.batch_ref, bf16[64,16384]{1,0:T(8,128)(2,1)} %x_ref.5, bf16[64,16384]{1,0:T(8,128)(2,1)} %y_ref.5, ...), custom_call_target="tpu_custom_call" | custom-call | tf_op jit(solution)/shard_map/pallas_call | solution.py:471
  110.6 0.0 copy-start
  110.6 2.2 %copy-done = f32[64,16384]{1,0:T(8,128)S(1)} copy-done((f32[64,16384]{1,0:T(8,128)S(1)}, f32[64,16384]{1,0:T(8,128)}, u32[]{:S(2)}) %copy-start) | copy-done | bytes 4194328
  112.8 0.0 copy-start.1
  112.8 1.0 copy-done.1
  113.8 69.8 %shard_map.116 = (f32[64,16384]{1,0:T(8,128)S(1)}, f32[32,128]{1,0:T(8,128)S(1)}) custom-call(f32[64,16384]{1,0:T(8,128)S(1)} %copy-done, f32[32,32,128]{2,1,0:T(8,128)S(1)} %copy-done.1), custom_call_target="tpu_custom_call" | custom-call | tf_op jit(solution)/shard_map/pallas_call | solution.py:381
  183.6 0.1 fusion.7
  183.6 0.6 maximum_bitcast_fusion
  184.3 2.0 %copy.14 = f32[64,16384]{1,0:T(8,128)} copy(f32[64,16384]{1,0:T(8,128)S(1)} %get-tuple-element.44) | data formatting | bytes 8388608
Async XLA Ops:
  110.6 2.2 %copy-start = (f32[64,16384]{1,0:T(8,128)S(1)}, f32[64,16384]{1,0:T(8,128)}, u32[]{:S(2)}) copy-start(f32[64,16384]{1,0:T(8,128)} %get-tuple-element.32.dy_in) | copy-start | bytes 12582916
  112.8 1.0 copy-start.1
